TPU v7x, 32 devices: a whole 2x2x4 slice. The times are simulated.
32 devices in a mesh: rows: 8 (over z, y), vecs: 4 (over x, core).
Axes of the slice: x: 2, y: 2, z: 4, core: 2. Of those that a mesh axis runs over, the one named last changes fastest.
Arguments:
- vectors: bfloat16 [32768, 1024], P('rows', 'vecs'), may hold values from -6 to 6, as said below
- blocks: bfloat16 [256, 5, 128, 128], P('rows'), may hold values from -0.25 to 0.25
- columns: int32 [256, 5], P('rows'), may hold values from 0 to 255, as said below
Outputs:
- basis: float32 [32768, 1024], P('rows', 'vecs')
Inputs may be any that keep to these rules, and one draw needn't show every extreme that they name: Each block row i names 5 block columns of the form i + d clipped to 0 .. 255, with distinct d in -8 .. 8; near the grid's ends some may repeat. `vectors`: entries of order one.
All inputs are finite; a program needn't handle non-finite values.
Results may differ from a plain program's by a relative error of at most 0.0075.
Values may be sent and summed in bfloat16 or wider, within the bound.
A program may use at most 128 MiB of HBM per device.

v0:
```python
import functools

import jax
import jax.numpy as jnp
from jax import lax
from jax.experimental import pallas as pl
from jax.experimental.pallas import tpu as pltpu
from jax.sharding import PartitionSpec as P

DEGREE = 4

filter_center = 0.25
filter_radius = 1.25

VMEM_LIMIT = 56 * 1024 * 1024


def factor_block(block, middle=None):
    size = block.shape[0]
    tiles = [block[8 * t : 8 * (t + 1), :] for t in range(size // 8)]
    lane = lax.broadcasted_iota(jnp.int32, (8, size), 1)
    sub = lax.broadcasted_iota(jnp.int32, (8, size), 0)

    def spread(array):
        return jnp.broadcast_to(array, (8, size))

    for first in range(size // 8):
        if middle and first == size // 16:
            middle()
        j = 8 * first
        each = range(8)
        at_any = jnp.logical_and(lane >= j, lane < j + 8)
        head = tiles[first]
        cols = [spread(head[:, j + a : j + a + 1]) for a in each]
        p = [[spread(cols[a][b : b + 1, :]) for a in range(b + 1)] for b in each]
        rows = [jnp.where(at_any, 0.0, spread(head[a : a + 1, :])) for a in each]
        rows = [jnp.where(lane == j + a, 1.0, rows[a]) for a in each]
        pairs, ready = [], []
        for a in range(0, 8, 2):
            b = a + 1
            det = p[a][a] * p[b][b] - p[b][a] * p[b][a]
            inv = 1.0 / det
            e_aa, e_ab, e_bb = p[b][b] * inv, p[b][a] * inv, p[a][a] * inv
            over = 1.0 / p[a][a]
            ready.append(rows[a] * lax.rsqrt(p[a][a]))
            ready.append((rows[b] - (p[b][a] * over) * rows[a]) * lax.rsqrt(det * over))
            mult = {}
            for c in range(b + 1, 8):
                mult[c, 0] = p[c][a] * e_aa - p[c][b] * e_ab
                mult[c, 1] = p[c][b] * e_bb - p[c][a] * e_ab
            for c in range(b + 1, 8):
                for d in range(b + 1, c + 1):
                    p[c][d] = p[c][d] - (mult[c, 0] * p[d][a] + mult[c, 1] * p[d][b])
            pairs.append((e_aa, e_ab, e_bb, mult, rows[a], rows[b]))
            for c in range(b + 1, 8):
                rows[c] = rows[c] - (mult[c, 0] * rows[a] + mult[c, 1] * rows[b])
        use = [None] * 8
        for number in reversed(range(4)):
            a, b = 2 * number, 2 * number + 1
            e_aa, e_ab, e_bb, mult, row_a, row_b = pairs[number]
            use[a] = e_aa * row_a - e_ab * row_b
            use[b] = e_bb * row_b - e_ab * row_a
            for c in range(b + 1, 8):
                use[a] = use[a] - mult[c, 0] * use[c]
                use[b] = use[b] - mult[c, 1] * use[c]
        for t in range(first + 1, size // 8):
            tile = tiles[t]
            cols = [spread(tile[:, j + a : j + a + 1]) for a in each]
            terms = [cols[a] * use[a] for a in each]
            while len(terms) > 1:
                terms = [x + y for x, y in zip(terms[::2], terms[1::2])]
            tiles[t] = jnp.where(at_any, 0.0, tile) - terms[0]
        top = ready[0]
        for a in range(1, 8):
            top = jnp.where(sub == a, ready[a], top)
        tiles[first] = top
    done = jnp.concatenate(tiles, axis=0)
    down = lax.broadcasted_iota(jnp.int32, (size, size), 0)
    across = lax.broadcasted_iota(jnp.int32, (size, size), 1)
    return jnp.where(across <= down, done, 0.0)


def halves(array):
    high = array.astype(jnp.bfloat16)
    return high, (array - high.astype(jnp.float32)).astype(jnp.bfloat16)


PLAIN = (((1,), (0,)), ((), ()))
TURNED = (((1,), (1,)), ((), ()))


def triple(left, right, dims):
    def one(a, b):
        return lax.dot_general(a, b, dims, preferred_element_type=jnp.float32)

    return one(left[0], right[0]) + (one(left[0], right[1]) + one(left[1], right[0]))


def gram_stages(rows, devices):
    stages, bit, held = [], 1, rows
    while bit < devices:
        halve = held % 16 == 0
        stages.append((bit, halve))
        held, bit = held // 2 if halve else held, bit * 2
    return stages


def flipped(index, bit):
    return index + bit - 2 * bit * lax.rem(index // bit, 2)


class Reduction:
    def __init__(self, stages, me, panel, total, landing, full, base, stage_sem, all_sem):
        self.me, self.panel, self.total, self.landing, self.full = me, panel, total, landing, full
        self.base, self.stage_sem, self.all_sem = base, stage_sem, all_sem
        self.near, self.over, self.side = flipped(panel, 1), flipped(panel, 2), panel // 2
        self.steps, self.shared = [], []
        start, held, taken = 0, total.shape[0], 0
        for bit, halve in stages:
            size = held // 2 if halve else held
            upper = lax.rem(me // bit, 2)
            keep = pl.multiple_of(start + upper * size, 8) if halve else start
            give = pl.multiple_of(start + (1 - upper) * size, 8) if halve else start
            self.steps.append((bit, size, keep, give, taken))
            start, held, taken = keep, size, taken + size
        self.start, self.held = start, held
        self.gathers = [n for n in reversed(range(len(stages))) if stages[n][1]]

    def reduce_copy(self, number):
        bit, size, _, give, taken = self.steps[number]
        return pltpu.make_async_remote_copy(
            src_ref=self.total.at[pl.ds(give, size)], dst_ref=self.landing.at[taken : taken + size],
            send_sem=self.stage_sem.at[0, number], recv_sem=self.stage_sem.at[1, number],
            device_id={"rows": flipped(self.me, bit)},
        )

    def reduce_start(self, number):
        if number < len(self.steps):
            self.reduce_copy(number).start()

    def reduce_finish(self, number):
        if number < len(self.steps):
            _, size, keep, _, taken = self.steps[number]
            self.reduce_copy(number).wait()
            self.total[pl.ds(keep, size), :] += self.landing[taken : taken + size, :]

    def piece(self, which, first, size):
        return self.full.at[which, pl.ds(pl.multiple_of(self.base + first, 8), size)]

    def hand(self, which, kind, number, first, size, peer):
        piece = self.piece(which, first, size)
        return pltpu.make_async_remote_copy(
            src_ref=piece, dst_ref=piece, send_sem=self.all_sem.at[0, kind, number],
            recv_sem=self.all_sem.at[1, kind, number], device_id={"vecs": peer},
        )

    def hands(self, number, kind):
        first, size = self.shared[number]
        which = self.over if kind == 2 else self.panel
        peer = self.near if kind else self.over
        return self.hand(which, kind, number, first, size, peer)

    def share(self, first, size):
        self.shared.append((first, size))
        number = len(self.shared) - 1

        @pl.when(self.side == 0)
        def _():
            self.hands(number, 0).start()

        self.hands(number, 1).start()

    def publish(self):
        rows = pl.ds(pl.multiple_of(self.base + self.start, 8), self.held)
        self.full[self.panel, rows, :] = self.total[pl.ds(self.start, self.held), :]
        self.share(self.start, self.held)

    def gather_copy(self, index):
        number = self.gathers[index]
        bit, size, keep, _, _ = self.steps[number]
        piece = self.piece(self.panel, keep, size)
        return pltpu.make_async_remote_copy(
            src_ref=piece, dst_ref=piece, send_sem=self.stage_sem.at[2, number],
            recv_sem=self.stage_sem.at[3, number], device_id={"rows": flipped(self.me, bit)},
        )

    def gather_start(self, index):
        if index < len(self.gathers):
            self.gather_copy(index).start()

    def gather_finish(self, index):
        if index < len(self.gathers):
            self.gather_copy(index).wait()
            _, size, _, give, _ = self.steps[self.gathers[index]]
            self.share(give, size)

    def settle(self):
        for number in range(len(self.shared)):

            @pl.when(self.side == 1)
            def _():
                self.hands(number, 0).wait_recv()
                self.hands(number, 2).start()

            @pl.when(self.side == 0)
            def _():
                self.hands(number, 0).wait_send()

            self.hands(number, 1).wait()

    def close(self):
        @pl.when(self.side == 1)
        def _():
            for number in range(len(self.shared)):
                self.hands(number, 2).wait()


def filter_kernel(
    near_stages, cross_stages, place_ref, vectors_ref, blocks_ref, sums_ref, block_ref, lead_ref,
    first_win, even_win, odd_win, tops, bottoms, even, odd, held,
    block, cross, near_total, cross_total, full, near_landing, cross_landing, cross_in, work, lead,
    in_sem, send_sem, recv_sem, copy_sem, keep_sem, swap_sem, side_sem, x_sem, pass_sem, rest_sem, on_sem,
    near_stage_sem, near_all_sem, cross_stage_sem, cross_all_sem,
):
    me, count = lax.axis_index("rows"), lax.axis_size("rows")
    panel = lax.axis_index("vecs")
    core, side = lax.rem(panel, 2), panel // 2
    near, over = flipped(panel, 1), flipped(panel, 2)
    beyond = flipped(over, 1)
    block_rows, nnz = blocks_ref.shape[:2]
    wide = block.shape[3]
    short = wide // 2
    reach = block_rows // 4
    span, part = 2 * reach, reach // 2
    windows = [first_win, odd_win, even_win, odd_win]
    states = [None, even, odd, even]
    above, below = me < count - 1, me > 0

    peers = [{"vecs": near}, {"vecs": over}] + [{"rows": flipped(me, bit)} for bit, _ in near_stages]
    inside = jnp.logical_and(above, below)
    for peer in peers:
        pl.semaphore_signal(pltpu.get_barrier_semaphore(), 1, device_id=peer)

    @pl.when(inside)
    def _():
        other = me - 1 + 2 * lax.rem(me, 2)
        pl.semaphore_signal(pltpu.get_barrier_semaphore(), 1, device_id={"rows": other})

    pieces = [
        (vectors_ref, first_win),
        (vectors_ref.at[:span], tops[0][0].at[part:]),
        (vectors_ref.at[: reach + part], tops[0][1].at[reach:]),
        (vectors_ref.at[span:], bottoms[0][0].at[:span]),
        (vectors_ref.at[span + part :], bottoms[0][1].at[: reach + part]),
        (blocks_ref, held),
    ]
    fetches = [pltpu.make_async_copy(*pair, in_sem.at[n]) for n, pair in enumerate(pieces)]
    for fetch in fetches:
        fetch.start()

    @pl.when(inside)
    def _():
        pl.semaphore_wait(pltpu.get_barrier_semaphore(), len(peers) + 1)

    @pl.when(jnp.logical_not(inside))
    def _():
        pl.semaphore_wait(pltpu.get_barrier_semaphore(), len(peers))

    def to_lower(step, far):
        source = vectors_ref if step == 0 else windows[step]
        return pltpu.make_async_remote_copy(
            src_ref=source.at[far * part : (far + 1) * part],
            dst_ref=bottoms[step % 2][far].at[span:],
            send_sem=send_sem.at[0, far, step % 2], recv_sem=recv_sem.at[0, far, step % 2],
            device_id={"rows": me - 1},
        )

    def to_upper(step, far):
        source = vectors_ref if step == 0 else windows[step]
        first = block_rows - (far + 1) * part
        return pltpu.make_async_remote_copy(
            src_ref=source.at[first : first + part], dst_ref=tops[step % 2][far].at[:part],
            send_sem=send_sem.at[1, far, step % 2], recv_sem=recv_sem.at[1, far, step % 2],
            device_id={"rows": me + 1},
        )

    def join_bottom(step):
        close, far = bottoms[step % 2]
        return pltpu.make_async_copy(close.at[span:], far.at[reach + part : span], copy_sem.at[0])

    def join_top(step):
        close, far = tops[step % 2]
        return pltpu.make_async_copy(close.at[:part], far.at[part:reach], copy_sem.at[1])

    def compute(step, start, rows, window):
        slot = (step + 1) % 2
        for row in range(start, start + rows):
            left = jnp.concatenate([held[row, j] for j in range(nnz)], axis=1)
            right = jnp.concatenate([window[place_ref[row, j]] for j in range(nnz)], axis=0)
            acc = jnp.dot(left, right, preferred_element_type=jnp.float32)
            cur = first_win[row].astype(jnp.float32) if step == 0 else states[step][row]
            new = (acc - filter_center * cur) * (1.0 / filter_radius)
            if step == 1:
                new = 2.0 * new - first_win[row].astype(jnp.float32)
            elif step > 1:
                new = 2.0 * new - states[step - 1][row]
            rounded = new.astype(jnp.bfloat16)
            if step == DEGREE - 1:
                block[panel, row] = rounded
                continue
            windows[step + 1][row] = rounded
            states[step + 1][row] = new
            if row < span:
                tops[slot][0][row + part] = rounded
            if row < reach + part:
                tops[slot][1][row + reach] = rounded
            if row >= span:
                bottoms[slot][0][row - span] = rounded
            if row >= span + part:
                bottoms[slot][1][row - span - part] = rounded

    def send(which, start, size, sems, number, peer):
        piece = block.at[which, pl.ds(start, size)]
        return pltpu.make_async_remote_copy(
            src_ref=piece, dst_ref=piece, send_sem=sems.at[0, number],
            recv_sem=sems.at[1, number], device_id={"vecs": peer},
        )

    def part_start(half, number):
        return half * 3 * reach if number else reach + half * reach

    to_over = [send(panel, part_start(1 - side, n), reach, x_sem, n, over) for n in range(2)]
    passed = [send(over, part_start(side, n), reach, pass_sem, n, near) for n in range(2)]
    rest = [send(panel, part_start(0, n), reach, rest_sem, n, over) for n in range(2)]
    onward = [send(over, part_start(0, n), reach, on_sem, n, near) for n in range(2)]
    to_near = [
        send(panel, first, size, side_sem, n, near)
        for n, (first, size) in enumerate(((reach, span), (3 * reach, reach), (0, reach)))
    ]
    contract = (((0,), (0,)), ((), ()))

    def product(left, right):
        return lax.dot_general(left, right, contract, preferred_element_type=jnp.float32)

    def rows_of(which, start, size):
        return block[which, pl.ds(start, size)].reshape(size * block.shape[2], wide)

    def add_own(start, size):
        @pl.loop(0, size // part)
        def _(index):
            own = rows_of(panel, start + index * part, part)
            near_total[:wide, :] += product(own, own)

    def add_near(start, size):
        @pl.loop(0, size // part)
        def _(index):
            own = rows_of(panel, start + index * part, part)
            beside = rows_of(near, start + index * part, part)

            @pl.when(core == 0)
            def _():
                near_total[wide:, :] += product(beside[:, :short], own)

            @pl.when(core == 1)
            def _():
                near_total[wide:, :] += product(own[:, short:], beside)

    def add_across(number):
        @pl.loop(0, 2)
        def _(index):
            start = part_start(side, number) + index * part
            own, there = rows_of(panel, start, part), rows_of(over, start, part)

            @pl.when(side == 0)
            def _():
                cross[core] += product(there, own)

            @pl.when(side == 1)
            def _():
                cross[core] += product(own, there)
                cross[1 - core] += product(rows_of(near, start, part), there)

    def add_beyond(number):
        @pl.when(side == 0)
        def _():
            @pl.loop(0, 2)
            def _(index):
                start = part_start(0, number) + index * part
                cross[1 - core] += product(rows_of(beyond, start, part), rows_of(panel, start, part))

    @pl.when(below)
    def _():
        to_lower(0, 0).start()

    @pl.when(above)
    def _():
        to_upper(0, 0).start()

    near_total[...] = jnp.zeros_like(near_total)
    cross[...] = jnp.zeros_like(cross)
    for fetch in fetches:
        fetch.wait()

    for step in range(DEGREE):
        last = step == DEGREE - 1
        compute(step, reach, reach, windows[step])
        compute(step, span, reach, windows[step])
        if last:
            to_over[0].start()
            to_near[0].start()

        @pl.when(below)
        def _():
            to_lower(step, 0).wait_send()
            to_lower(step, 1).start()

        @pl.when(above)
        def _():
            to_upper(step, 0).wait_send()
            to_upper(step, 1).start()

        if last:
            add_own(reach, span)

        @pl.when(above)
        def _():
            to_lower(step, 0).wait_recv()
            join_bottom(step).start()

        compute(step, 3 * reach, part, bottoms[step % 2][0])

        @pl.when(below)
        def _():
            to_upper(step, 0).wait_recv()
            join_top(step).start()

        compute(step, part, part, tops[step % 2][0])
        if last:
            to_over[0].wait_send()

            @pl.when(side == 0)
            def _():
                rest[0].start()

        @pl.when(above)
        def _():
            join_bottom(step).wait()
            to_lower(step, 1).wait_recv()

        compute(step, 3 * reach + part, part, bottoms[step % 2][1])
        if last:
            to_near[1].start()

            @pl.when(side == 0)
            def _():
                to_over[1].start()
        else:

            @pl.when(above)
            def _():
                to_upper(step + 1, 0).start()

        @pl.when(below)
        def _():
            join_top(step).wait()
            to_upper(step, 1).wait_recv()

        compute(step, 0, part, tops[step % 2][1])
        if last:
            to_near[2].start()

            @pl.when(side == 1)
            def _():
                to_over[1].start()
        else:

            @pl.when(below)
            def _():
                to_lower(step + 1, 0).start()

        @pl.when(below)
        def _():
            to_lower(step, 1).wait_send()

        @pl.when(above)
        def _():
            to_upper(step, 1).wait_send()

    keep_own = pltpu.make_async_copy(block.at[panel], block_ref.at[panel], keep_sem.at[0])
    keep_own.start()
    add_own(3 * reach, reach)
    add_own(0, reach)
    to_near[0].wait()
    add_near(reach, span)
    to_near[1].wait()
    add_near(3 * reach, reach)
    to_near[2].wait()
    add_near(0, reach)
    keep_near = pltpu.make_async_copy(block.at[near], block_ref.at[near], keep_sem.at[1])
    keep_near.start()

    shape = (me, panel)
    near_sum = Reduction(near_stages, *shape, near_total, near_landing, full, 0, near_stage_sem, near_all_sem)
    cross_sum = Reduction(
        cross_stages, *shape, cross_total, cross_landing, full, wide + short, cross_stage_sem, cross_all_sem
    )
    stages = len(near_stages)
    ahead = min(stages, 3)
    near_sum.reduce_start(0)
    to_over[0].wait_recv()
    passed[0].start()
    add_across(0)
    for number in range(stages):
        near_sum.reduce_finish(number)
        near_sum.reduce_start(number + 1)
        if number == 0:
            passed[0].wait()
            add_beyond(0)
    near_sum.publish()
    near_sum.gather_start(0)
    to_over[1].wait()
    passed[1].start()
    add_across(1)
    passed[1].wait()
    add_beyond(1)
    swap = pltpu.make_async_remote_copy(
        src_ref=cross.at[1 - side], dst_ref=cross_in,
        send_sem=swap_sem.at[0], recv_sem=swap_sem.at[1], device_id={"vecs": over},
    )
    swap.start()
    near_sum.gather_finish(0)
    near_sum.gather_start(1)
    swap.wait()
    cross_total[...] = cross[side] + cross_in[...]
    cross_sum.reduce_start(0)
    for number in range(1, stages):
        near_sum.gather_finish(number)
        near_sum.gather_start(number + 1)
        if number == 1:
            cross_sum.reduce_finish(0)
            cross_sum.reduce_start(1)
    near_sum.settle()
    near_sum.close()

    @pl.when(side == 0)
    def _():
        rest[0].wait_send()
        rest[1].start()

    def gather_next(number):
        cross_sum.gather_finish(number)
        cross_sum.gather_start(number + 1)

    def reduced():
        cross_sum.reduce_finish(2)
        for number in range(3, stages):
            cross_sum.reduce_start(number)
            cross_sum.reduce_finish(number)
        cross_sum.publish()
        cross_sum.gather_start(0)

    def reduce_second():
        cross_sum.reduce_finish(1)
        cross_sum.reduce_start(2)

    def pass_rest():
        @pl.when(side == 1)
        def _():
            for copy, pass_on in zip(rest, onward):
                copy.wait_recv()
                pass_on.start()

    later = [functools.partial(gather_next, n) for n in range(1, len(cross_sum.gathers))]
    actions = [
        [reduce_second], [reduced], [functools.partial(gather_next, 0)], later[:1], later[1:], [],
        [pass_rest], [cross_sum.settle],
    ]
    lead_factor(full, work, lead, actions)
    lead_copy = pltpu.make_async_copy(lead, lead_ref, copy_sem.at[0])
    lead_copy.start()
    keep_own.wait()
    keep_near.wait()
    keep_over = pltpu.make_async_copy(block.at[over], block_ref.at[over], keep_sem.at[0])
    keep_beyond = pltpu.make_async_copy(block.at[beyond], block_ref.at[beyond], keep_sem.at[1])

    @pl.when(side == 0)
    def _():
        rest[1].wait_send()

    @pl.when(side == 1)
    def _():
        keep_over.start()

    cross_sum.close()
    low_sums = pltpu.make_async_copy(full.at[:2], sums_ref.at[:2], keep_sem.at[2])
    high_sums = pltpu.make_async_copy(full.at[2:], sums_ref.at[2:], keep_sem.at[3])
    low_sums.start()

    @pl.when(side == 1)
    def _():
        high_sums.start()
        onward[0].wait()
        onward[1].wait()
        keep_beyond.start()
        keep_over.wait()
        keep_beyond.wait()
        high_sums.wait()

    low_sums.wait()
    lead_copy.wait()


def filtered_sums(vectors, blocks, columns):
    rows, width = vectors.shape
    block_rows, nnz, size_b = blocks.shape[:3]
    panels, devices = lax.axis_size("vecs"), lax.axis_size("rows")
    reach = block_rows // 4
    part = reach // 2
    near_rows, cross_rows = width + width // 2, width
    near_stages, cross_stages = gram_stages(near_rows, devices), gram_stages(cross_rows, devices)
    steps = len(near_stages)
    row = lax.broadcasted_iota(jnp.int32, columns.shape, 0)
    shift = jnp.zeros_like(columns)
    for start, amount in (
        (0, reach), (part, part), (reach, 0), (3 * reach, -2 * reach), (3 * reach + part, -2 * reach - part),
    ):
        shift = jnp.where(row >= start, amount, shift)
    place = columns - lax.axis_index("rows") * block_rows + shift
    window = pltpu.VMEM((block_rows, size_b, width), jnp.bfloat16)
    side = pltpu.VMEM((2 * reach + part, size_b, width), jnp.bfloat16)
    state = pltpu.VMEM((block_rows, size_b, width), jnp.float32)
    anywhere = pl.BlockSpec(memory_space=pl.ANY)
    dma = pltpu.SemaphoreType.DMA

    def single(tall):
        return pltpu.VMEM((tall, width), jnp.float32)

    def kernel(*refs):
        inputs, wins, refs = refs[:6], refs[6:9], refs[9:]
        tops = ((refs[0], refs[1]), (refs[2], refs[3]))
        bottoms = ((refs[4], refs[5]), (refs[6], refs[7]))
        filter_kernel(near_stages, cross_stages, *inputs, *wins, tops, bottoms, *refs[8:])

    sums, block, lead = pl.pallas_call(
        kernel,
        out_shape=[
            jax.ShapeDtypeStruct((panels, near_rows + cross_rows, width), jnp.float32),
            jax.ShapeDtypeStruct((panels, block_rows, size_b, width), jnp.bfloat16),
            jax.ShapeDtypeStruct((2 * width, 2 * width), jnp.float32),
        ],
        in_specs=[pl.BlockSpec(memory_space=pltpu.SMEM), anywhere, anywhere],
        out_specs=[anywhere] * 3,
        scratch_shapes=[window] * 3 + [side] * 8 + [state] * 2 + [
            pltpu.VMEM(blocks.shape, jnp.bfloat16),
            pltpu.VMEM((panels, block_rows, size_b, width), jnp.bfloat16),
            pltpu.VMEM((2, width, width), jnp.float32),
            single(near_rows), single(cross_rows),
            pltpu.VMEM((panels, near_rows + cross_rows, width), jnp.float32),
            single(2 * near_rows), single(2 * cross_rows), single(width),
            pltpu.VMEM((2 * width, 2 * width), jnp.float32),
            pltpu.VMEM((2 * width, 2 * width), jnp.float32),
            dma((6,)), dma((2, 2, 2)), dma((2, 2, 2)), dma((2,)), dma((4,)), dma((2,)),
            dma((2, 3)), dma((2, 2)), dma((2, 2)), dma((2, 2)), dma((2, 2)),
            dma((4, steps)), dma((2, 3, steps + 1)), dma((4, steps)), dma((2, 3, steps + 1)),
        ],
        compiler_params=pltpu.CompilerParams(
            vmem_limit_bytes=VMEM_LIMIT, collective_id=0, has_side_effects=True
        ),
    )(place, vectors.reshape(block_rows, size_b, width), blocks)
    return sums, block.reshape(panels, rows, width), lead


def scales(diagonal):
    wide = diagonal.shape[0]
    down = lax.broadcasted_iota(jnp.int32, (wide, wide), 0)
    across = lax.broadcasted_iota(jnp.int32, (wide, wide), 1)
    kept = jnp.where(down == across, diagonal, 0.0)
    sums = jnp.sum(kept, axis=0, keepdims=True)
    return lax.rsqrt(jnp.sum(kept, axis=1, keepdims=True)), lax.rsqrt(sums), sums


def fill_lower(full, first, work):
    wide = full.shape[2]
    short = wide // 2
    parts = [scales(full[first + n, :wide, :]) for n in range(2)]
    for n in range(2):
        own = slice(n * wide, (n + 1) * wide)
        work[own, own] = full[first + n, :wide, :] * parts[n][0] * parts[n][1]
        rows = slice(n * short, (n + 1) * short)
        below = wide + n * short
        work[below : below + short, :wide] = (
            full[first + n, wide : wide + short, :] * parts[1][0][rows, :] * parts[0][1]
        )
    return parts


def lead_factor(full, work, lead, actions):
    whole = work.shape[0]
    wide, size = whole // 2, whole // 4
    work[:wide, wide:] = jnp.zeros((wide, wide), jnp.float32)
    fill_lower(full, 0, work)

    @pl.loop(0, 4)
    def _(k):
        start = pl.multiple_of(k * size, size)
        at = pl.ds(start, size)

        def act(second):
            for n in range(4):

                @pl.when(k == n)
                def _():
                    for action in actions[2 * n + second]:
                        action()

        done = factor_block(work[at, at], functools.partial(act, 0))
        act(1)
        lower = halves(done)
        rows = lax.broadcasted_iota(jnp.int32, (whole, size), 0)
        cols = lax.broadcasted_iota(jnp.int32, (size, whole), 1)
        below = rows >= start + size
        own = work[:, at]
        column = jnp.where(below, triple(halves(own), lower, TURNED), 0.0)
        known = jnp.where(cols < start, work[at, :], 0.0)
        lead[at, :] = triple(lower, halves(known), PLAIN)
        lead[at, at] = done
        work[:, at] = jnp.where(below, 0.0, own)
        pieces = halves(column)
        work[...] -= triple(pieces, halves(lead[at, :]), PLAIN) + triple(pieces, pieces, TURNED)


def trail_factor(work, inverse, size):
    full = work.shape[0]
    count = full // size

    def span(c):
        return slice(c * size, (c + 1) * size)

    done = factor_block(work[span(0), span(0)])
    for c in range(count):
        own = span(c)
        lower = halves(done)
        inverse[own, own] = done
        if c + 1 < count:
            inverse[own, (c + 1) * size :] = jnp.zeros((size, full - (c + 1) * size), jnp.float32)
            below = slice((c + 1) * size, full)
            column = triple(halves(work[below, own]), lower, TURNED)
            pieces = halves(column)
            top = (pieces[0][:size], pieces[1][:size])
            following = work[span(c + 1), span(c + 1)] - triple(top, top, TURNED)
        if c > 0:
            known = triple(lower, halves(work[own, : c * size]), PLAIN)
            inverse[own, : c * size] = known
        if c + 1 < count:
            done = factor_block(following)
            work[below, own] = -triple(pieces, lower, PLAIN)
            if c > 0:
                work[below, : c * size] -= triple(pieces, halves(known), PLAIN)
            for j in range(c + 1, count):
                first = max(j, c + 2)
                if first == count:
                    continue
                rows = slice((first - c - 1) * size, (count - c - 1) * size)
                cols = slice((j - c - 1) * size, (j - c) * size)
                work[first * size :, span(j)] -= triple(
                    (pieces[0][rows], pieces[1][rows]), (pieces[0][cols], pieces[1][cols]), TURNED
                )


def finish_kernel(
    size, total_rows, sums_ref, lead_ref, block_ref, out_ref,
    work, inverse, cross, mixed, factor, block, result, in_sem, out_sem,
):
    panels, _, wide = sums_ref.shape
    short = wide // 2
    mine = lax.axis_index("vecs")
    side = mine // 2

    def fetch(panel):
        return pltpu.make_async_copy(block_ref.at[panel], block.at[panel], in_sem.at[panel])

    for panel in range(panels):

        @pl.when(panel <= mine)
        def _():
            fetch(panel).start()

    def scaled(sums):
        return lax.rsqrt(sums * (1.0 / total_rows))

    parts = [scales(sums_ref[panel, :wide, :]) for panel in range(2)]
    left_scale = jnp.concatenate([scaled(part[2]) for part in parts], axis=1)

    def keep(rows, first):
        high, low = halves(rows)
        factor[0, :, first : first + 2 * wide] = high
        factor[1, :, first : first + 2 * wide] = low

    @pl.when(side == 0)
    def _():
        keep(lead_ref[pl.ds(pl.multiple_of(mine * wide, wide), wide), :] * left_scale, 0)

    @pl.when(side == 1)
    def _():
        later = fill_lower(sums_ref, 2, work)
        for panel in range(panels):
            core, row = panel % 2, panel // 2
            cross[row * wide : (row + 1) * wide, core * wide : (core + 1) * wide] = (
                sums_ref[panel, wide + short :, :] * later[row][0] * parts[core][1]
            )
        lead = halves(lead_ref[...])
        ratio = halves(triple(halves(cross[...]), lead, TURNED))
        upper = (ratio[0][:wide], ratio[1][:wide])
        lower = (ratio[0][wide:], ratio[1][wide:])
        work[:wide, :wide] -= triple(upper, upper, TURNED)
        work[wide:, :] -= triple(lower, ratio, TURNED)
        mixed[...] = triple(ratio, lead, PLAIN)
        trail_factor(work, inverse, size)
        own = inverse[pl.ds(pl.multiple_of((mine - 2) * wide, wide), wide), :]
        keep(-triple(halves(own), halves(mixed[...]), PLAIN) * left_scale, 0)
        keep(own * jnp.concatenate([scaled(part[2]) for part in later], axis=1), 2 * wide)

    tiles = out_sem.shape[0]
    tile = block.shape[1] // tiles

    def store(index):
        rows = pl.ds(pl.multiple_of(index * tile, tile), tile)
        return pltpu.make_async_copy(result.at[rows], out_ref.at[rows], out_sem.at[index])

    for number in range(1, panels + 1):

        @pl.when(mine == number - 1)
        def _():
            for panel in range(number):
                fetch(panel).wait()
            deep = number * wide
            right = jnp.concatenate([factor[0, :, :deep], factor[1, :, :deep]], axis=1)

            @pl.loop(0, tiles)
            def _(index):
                rows = pl.ds(pl.multiple_of(index * tile, tile), tile)
                left = jnp.concatenate([block[panel, rows, :] for panel in range(number)] * 2, axis=1)
                result[rows, :] = lax.dot_general(
                    left, right, TURNED, preferred_element_type=jnp.float32
                )
                store(index).start()

    for index in range(tiles):
        store(index).wait()


def finish(sums, block, lead, total_rows):
    panels, rows, wide = block.shape
    size = 128
    tiles = 4
    anywhere = pl.BlockSpec(memory_space=pl.ANY)
    near = pl.BlockSpec(memory_space=pltpu.VMEM)
    square = pltpu.VMEM((2 * wide, 2 * wide), jnp.float32)
    return pl.pallas_call(
        functools.partial(finish_kernel, size, total_rows),
        out_shape=jax.ShapeDtypeStruct((rows, wide), jnp.float32),
        in_specs=[near, near, anywhere],
        out_specs=anywhere,
        scratch_shapes=[square] * 4 + [
            pltpu.VMEM((2, wide, panels * wide), jnp.bfloat16),
            pltpu.VMEM((panels, rows, wide), jnp.bfloat16),
            pltpu.VMEM((rows, wide), jnp.float32),
            pltpu.SemaphoreType.DMA((panels,)),
            pltpu.SemaphoreType.DMA((tiles,)),
        ],
        compiler_params=pltpu.CompilerParams(vmem_limit_bytes=VMEM_LIMIT),
    )(sums, lead, block)


def shards(vectors, blocks, columns):
    total_rows = vectors.shape[0] * lax.axis_size("rows")
    sums, block, lead = filtered_sums(vectors, blocks, columns)
    return finish(sums, block, lead, total_rows)


def solution(mesh):
    in_specs = (P("rows", "vecs"), P("rows", None, None, None), P("rows", None))
    out_specs = P("rows", "vecs")
    return jax.shard_map(shards, mesh=mesh, in_specs=in_specs, out_specs=out_specs, check_vma=False)
```

profile of v0, /device:TPU:3, one launch (start us, length us, event | category | flops | bytes accessed | tf_op | source)
XLA Modules:
  0.0 211.4 jit_solution(3564609647023062478)
XLA Ops:
  0.0 0.8 copy.5
  0.8 0.7 select_add_fusion.refs_0_
  1.5 177.7 %shard_map.37 = (f32[4,640,256]{2,1,0:T(8,128)}, bf16[4,32,128,256]{3,2,1,0:T(8,128)(2,1)}, f32[512,512]{1,0:T(8,128)}) custom-call(s32[32,5]{1,0:T(8,128)} %select_add_fusion.refs_0_, bf16[32,128,256]{2,1,0:T(8,128)(2,1)} %bitcast.3, bf16[32,5,128,128]{3,2,1,0:T(8,128)(2,1)} %refs_2_.1), custom_call_target="tpu_custom_call" | custom-call | tf_op jit(solution)/shard_map/pallas_call | solution.py:644
  179.2 31.9 %shard_map.38 = f32[4096,256]{1,0:T(8,128)} custom-call(f32[4,640,256]{2,1,0:T(8,128)} %get-tuple-element.8.sums_ref, f32[512,512]{1,0:T(8,128)} %get-tuple-element.9.lead_ref, bf16[4,4096,256]{2,1,0:T(8,128)(2,1)} %bitcast.2), custom_call_target="tpu_custom_call" | custom-call | tf_op jit(solution)/shard_map/pallas_call | solution.py:859
  (3 shorter events, 0.0 us)
where the time goes:
time: 212 us; the launch traced here: 211 us
  Pallas kernels  210 us (99%)
    pallas_call x1, Pallas kernels, filtered_sums(): pl.pallas_call(kernel, out_shape=[jax.ShapeDtypeStruct((panels, near_rows...  178 us
    pallas_call x1, Pallas kernels, finish(): pl.pallas_call(functools.partial(finish_kernel, size, total_rows), out_sh...  31.9 us

commit v1 on v0

--- a/solution.py
+++ b/solution.py
@@ -218,7 +218,7 @@
 def filter_kernel(
     near_stages, cross_stages, place_ref, vectors_ref, blocks_ref, sums_ref, block_ref, lead_ref,
     first_win, even_win, odd_win, tops, bottoms, even, odd, held,
-    block, cross, near_total, cross_total, full, near_landing, cross_landing, cross_in, work, lead,
+    block, cross, near_acc, near_total, cross_total, full, near_landing, cross_landing, cross_in, work, lead,
     in_sem, send_sem, recv_sem, copy_sem, keep_sem, swap_sem, side_sem, x_sem, pass_sem, rest_sem, on_sem,
     near_stage_sem, near_all_sem, cross_stage_sem, cross_all_sem,
 ):
@@ -349,7 +349,7 @@
         @pl.loop(0, size // part)
         def _(index):
             own = rows_of(panel, start + index * part, part)
-            near_total[:wide, :] += product(own, own)
+            near_acc[:wide, :] += product(own, own)
 
     def add_near(start, size):
         @pl.loop(0, size // part)
@@ -359,11 +359,11 @@
 
             @pl.when(core == 0)
             def _():
-                near_total[wide:, :] += product(beside[:, :short], own)
+                near_acc[wide:, :] += product(beside[:, :short], own)
 
             @pl.when(core == 1)
             def _():
-                near_total[wide:, :] += product(own[:, short:], beside)
+                near_acc[wide:, :] += product(own[:, short:], beside)
 
     def add_across(number):
         @pl.loop(0, 2)
@@ -396,7 +396,7 @@
     def _():
         to_upper(0, 0).start()
 
-    near_total[...] = jnp.zeros_like(near_total)
+    near_acc[...] = jnp.zeros_like(near_acc)
     cross[...] = jnp.zeros_like(cross)
     for fetch in fetches:
         fetch.wait()
@@ -436,11 +436,18 @@
 
         compute(step, part, part, tops[step % 2][0])
         if last:
-            to_over[0].wait_send()
+            to_near[0].wait()
+            add_near(reach, span)
+            to_over[0].wait()
+            passed[0].start()
 
             @pl.when(side == 0)
             def _():
                 rest[0].start()
+
+            add_across(0)
+            passed[0].wait()
+            add_beyond(0)
 
         @pl.when(above)
         def _():
@@ -490,8 +497,6 @@
     keep_own.start()
     add_own(3 * reach, reach)
     add_own(0, reach)
-    to_near[0].wait()
-    add_near(reach, span)
     to_near[1].wait()
     add_near(3 * reach, reach)
     to_near[2].wait()
@@ -499,23 +504,23 @@
     keep_near = pltpu.make_async_copy(block.at[near], block_ref.at[near], keep_sem.at[1])
     keep_near.start()
 
+    quarter = short // 2
+    near_total[:short, :short] = near_acc[:short, :short]
+    near_total[:short, short:] = near_acc[short:wide, short:]
+    near_total[short : short + quarter, :short] = near_acc[short : short + quarter, :short]
+    near_total[short : short + quarter, short:] = near_acc[short + quarter : wide, :short]
+    near_total[short + quarter :, :] = near_acc[wide:, :]
     shape = (me, panel)
     near_sum = Reduction(near_stages, *shape, near_total, near_landing, full, 0, near_stage_sem, near_all_sem)
     cross_sum = Reduction(
-        cross_stages, *shape, cross_total, cross_landing, full, wide + short, cross_stage_sem, cross_all_sem
+        cross_stages, *shape, cross_total, cross_landing, full, near_total.shape[0], cross_stage_sem, cross_all_sem
     )
     stages = len(near_stages)
     ahead = min(stages, 3)
     near_sum.reduce_start(0)
-    to_over[0].wait_recv()
-    passed[0].start()
-    add_across(0)
     for number in range(stages):
         near_sum.reduce_finish(number)
         near_sum.reduce_start(number + 1)
-        if number == 0:
-            passed[0].wait()
-            add_beyond(0)
     near_sum.publish()
     near_sum.gather_start(0)
     to_over[1].wait()
@@ -575,7 +580,8 @@
         [reduce_second], [reduced], [functools.partial(gather_next, 0)], later[:1], later[1:], [],
         [pass_rest], [cross_sum.settle],
     ]
-    lead_factor(full, work, lead, actions)
+    fill_lower(full, 0, work)
+    square_factor(work, lead, block.shape[2], actions)
     lead_copy = pltpu.make_async_copy(lead, lead_ref, copy_sem.at[0])
     lead_copy.start()
     keep_own.wait()
@@ -616,7 +622,7 @@
     panels, devices = lax.axis_size("vecs"), lax.axis_size("rows")
     reach = block_rows // 4
     part = reach // 2
-    near_rows, cross_rows = width + width // 2, width
+    near_rows, cross_rows = width + width // 4, width
     near_stages, cross_stages = gram_stages(near_rows, devices), gram_stages(cross_rows, devices)
     steps = len(near_stages)
     row = lax.broadcasted_iota(jnp.int32, columns.shape, 0)
@@ -654,7 +660,7 @@
             pltpu.VMEM(blocks.shape, jnp.bfloat16),
             pltpu.VMEM((panels, block_rows, size_b, width), jnp.bfloat16),
             pltpu.VMEM((2, width, width), jnp.float32),
-            single(near_rows), single(cross_rows),
+            single(width + width // 2), single(near_rows), single(cross_rows),
             pltpu.VMEM((panels, near_rows + cross_rows, width), jnp.float32),
             single(2 * near_rows), single(2 * cross_rows), single(width),
             pltpu.VMEM((2 * width, 2 * width), jnp.float32),
@@ -681,62 +687,42 @@
 
 def fill_lower(full, first, work):
     wide = full.shape[2]
-    short = wide // 2
-    parts = [scales(full[first + n, :wide, :]) for n in range(2)]
+    short, quarter = wide // 2, wide // 4
+    parts = []
     for n in range(2):
-        own = slice(n * wide, (n + 1) * wide)
-        work[own, own] = full[first + n, :wide, :] * parts[n][0] * parts[n][1]
+        ends = [scales(full[first + n, :short, m * short : (m + 1) * short]) for m in range(2)]
+        parts.append([jnp.concatenate([end[axis] for end in ends], axis=min(axis, 1)) for axis in range(3)])
+        start = n * wide
+        for m in range(2):
+            own = slice(start + m * short, start + (m + 1) * short)
+            work[own, own] = full[first + n, :short, m * short : (m + 1) * short] * ends[m][0] * ends[m][1]
+            rows = slice(start + short + m * quarter, start + short + (m + 1) * quarter)
+            part = full[first + n, short : short + quarter, m * short : (m + 1) * short]
+            down = ends[1][0][m * quarter : (m + 1) * quarter, :]
+            work[rows, start : start + short] = part * down * ends[0][1]
+    for n in range(2):
         rows = slice(n * short, (n + 1) * short)
         below = wide + n * short
         work[below : below + short, :wide] = (
-            full[first + n, wide : wide + short, :] * parts[1][0][rows, :] * parts[0][1]
+            full[first + n, short + quarter : wide + quarter, :] * parts[1][0][rows, :] * parts[0][1]
         )
     return parts
 
 
-def lead_factor(full, work, lead, actions):
-    whole = work.shape[0]
-    wide, size = whole // 2, whole // 4
-    work[:wide, wide:] = jnp.zeros((wide, wide), jnp.float32)
-    fill_lower(full, 0, work)
-
-    @pl.loop(0, 4)
-    def _(k):
-        start = pl.multiple_of(k * size, size)
-        at = pl.ds(start, size)
-
-        def act(second):
-            for n in range(4):
-
-                @pl.when(k == n)
-                def _():
-                    for action in actions[2 * n + second]:
-                        action()
-
-        done = factor_block(work[at, at], functools.partial(act, 0))
-        act(1)
-        lower = halves(done)
-        rows = lax.broadcasted_iota(jnp.int32, (whole, size), 0)
-        cols = lax.broadcasted_iota(jnp.int32, (size, whole), 1)
-        below = rows >= start + size
-        own = work[:, at]
-        column = jnp.where(below, triple(halves(own), lower, TURNED), 0.0)
-        known = jnp.where(cols < start, work[at, :], 0.0)
-        lead[at, :] = triple(lower, halves(known), PLAIN)
-        lead[at, at] = done
-        work[:, at] = jnp.where(below, 0.0, own)
-        pieces = halves(column)
-        work[...] -= triple(pieces, halves(lead[at, :]), PLAIN) + triple(pieces, pieces, TURNED)
-
-
-def trail_factor(work, inverse, size):
+def square_factor(work, inverse, size, actions=()):
     full = work.shape[0]
     count = full // size
+    waiting = list(actions)
+
+    def act():
+        for action in waiting.pop(0) if waiting else []:
+            action()
 
     def span(c):
         return slice(c * size, (c + 1) * size)
 
-    done = factor_block(work[span(0), span(0)])
+    done = factor_block(work[span(0), span(0)], act)
+    act()
     for c in range(count):
         own = span(c)
         lower = halves(done)
@@ -752,7 +738,8 @@
             known = triple(lower, halves(work[own, : c * size]), PLAIN)
             inverse[own, : c * size] = known
         if c + 1 < count:
-            done = factor_block(following)
+            done = factor_block(following, act)
+            act()
             work[below, own] = -triple(pieces, lower, PLAIN)
             if c > 0:
                 work[below, : c * size] -= triple(pieces, halves(known), PLAIN)
@@ -788,8 +775,12 @@
     def scaled(sums):
         return lax.rsqrt(sums * (1.0 / total_rows))
 
-    parts = [scales(sums_ref[panel, :wide, :]) for panel in range(2)]
+    parts = []
+    for panel in range(2):
+        for m in range(2):
+            parts.append(scales(sums_ref[panel, :short, m * short : (m + 1) * short]))
     left_scale = jnp.concatenate([scaled(part[2]) for part in parts], axis=1)
+    along = [jnp.concatenate([part[1] for part in parts[2 * n : 2 * n + 2]], axis=1) for n in range(2)]
 
     def keep(rows, first):
         high, low = halves(rows)
@@ -806,7 +797,7 @@
         for panel in range(panels):
             core, row = panel % 2, panel // 2
             cross[row * wide : (row + 1) * wide, core * wide : (core + 1) * wide] = (
-                sums_ref[panel, wide + short :, :] * later[row][0] * parts[core][1]
+                sums_ref[panel, wide + short // 2 :, :] * later[row][0] * along[core]
             )
         lead = halves(lead_ref[...])
         ratio = halves(triple(halves(cross[...]), lead, TURNED))
@@ -815,7 +806,7 @@
         work[:wide, :wide] -= triple(upper, upper, TURNED)
         work[wide:, :] -= triple(lower, ratio, TURNED)
         mixed[...] = triple(ratio, lead, PLAIN)
-        trail_factor(work, inverse, size)
+        square_factor(work, inverse, size)
         own = inverse[pl.ds(pl.multiple_of((mine - 2) * wide, wide), wide), :]
         keep(-triple(halves(own), halves(mixed[...]), PLAIN) * left_scale, 0)
         keep(own * jnp.concatenate([scaled(part[2]) for part in later], axis=1), 2 * wide)

time: 212 us -> 228 us (1.075); the launches traced: 211 us -> 225 us
  Pallas kernels: 210 us -> 223 us
    pallas_call x1, Pallas kernels: 178 us -> 191 us  [filtered_sums(): pl.pallas_call(kernel, out_shape=[jax.ShapeDtypeStruct((panels, near_rows...]
where the time goes in v1:
time: 228 us; the launch traced here: 225 us
  Pallas kernels  223 us (98%)
    pallas_call x1, Pallas kernels, filtered_sums(): pl.pallas_call(kernel, out_shape=[jax.ShapeDtypeStruct((panels, near_rows...  191 us
    pallas_call x1, Pallas kernels, finish(): pl.pallas_call(functools.partial(finish_kernel, size, total_rows), out_sh...  31.5 us

profile of v1, /device:TPU:3, one launch (start us, length us, event | category | flops | bytes accessed | tf_op | source)
XLA Modules:
  0.0 224.7 jit_solution(6764383925001723981)
XLA Ops:
  0.0 0.8 copy.5
  0.8 0.7 select_add_fusion.refs_0_
  1.5 191.5 %shard_map.37 = (f32[4,576,256]{2,1,0:T(8,128)}, bf16[4,32,128,256]{3,2,1,0:T(8,128)(2,1)}, f32[512,512]{1,0:T(8,128)}) custom-call(s32[32,5]{1,0:T(8,128)} %select_add_fusion.refs_0_, bf16[32,128,256]{2,1,0:T(8,128)(2,1)} %bitcast.3, bf16[32,5,128,128]{3,2,1,0:T(8,128)(2,1)} %refs_2_.1), custom_call_target="tpu_custom_call" | custom-call | tf_op jit(solution)/shard_map/pallas_call | solution.py:650
  193.0 31.5 %shard_map.38 = f32[4096,256]{1,0:T(8,128)} custom-call(f32[4,576,256]{2,1,0:T(8,128)} %get-tuple-element.8.sums_ref, f32[512,512]{1,0:T(8,128)} %get-tuple-element.9.lead_ref, bf16[4,4096,256]{2,1,0:T(8,128)(2,1)} %bitcast.2), custom_call_target="tpu_custom_call" | custom-call | tf_op jit(solution)/shard_map/pallas_call | solution.py:850
  (3 shorter events, 0.0 us)

commit v2 on v1

--- a/solution.py
+++ b/solution.py
@@ -435,20 +435,6 @@
             join_top(step).start()
 
         compute(step, part, part, tops[step % 2][0])
-        if last:
-            to_near[0].wait()
-            add_near(reach, span)
-            to_over[0].wait()
-            passed[0].start()
-
-            @pl.when(side == 0)
-            def _():
-                rest[0].start()
-
-            add_across(0)
-            passed[0].wait()
-            add_beyond(0)
-
         @pl.when(above)
         def _():
             join_bottom(step).wait()
@@ -497,6 +483,8 @@
     keep_own.start()
     add_own(3 * reach, reach)
     add_own(0, reach)
+    to_near[0].wait()
+    add_near(reach, span)
     to_near[1].wait()
     add_near(3 * reach, reach)
     to_near[2].wait()
@@ -518,9 +506,20 @@
     stages = len(near_stages)
     ahead = min(stages, 3)
     near_sum.reduce_start(0)
+    to_over[0].wait()
+    passed[0].start()
+
+    @pl.when(side == 0)
+    def _():
+        rest[0].start()
+
+    add_across(0)
     for number in range(stages):
         near_sum.reduce_finish(number)
         near_sum.reduce_start(number + 1)
+        if number == 0:
+            passed[0].wait()
+            add_beyond(0)
     near_sum.publish()
     near_sum.gather_start(0)
     to_over[1].wait()
@@ -580,8 +579,7 @@
         [reduce_second], [reduced], [functools.partial(gather_next, 0)], later[:1], later[1:], [],
         [pass_rest], [cross_sum.settle],
     ]
-    fill_lower(full, 0, work)
-    square_factor(work, lead, block.shape[2], actions)
+    lead_factor(full, work, lead, actions)
     lead_copy = pltpu.make_async_copy(lead, lead_ref, copy_sem.at[0])
     lead_copy.start()
     keep_own.wait()
@@ -707,6 +705,41 @@
             full[first + n, short + quarter : wide + quarter, :] * parts[1][0][rows, :] * parts[0][1]
         )
     return parts
+
+
+def lead_factor(full, work, lead, actions):
+    whole = work.shape[0]
+    wide, size = whole // 2, whole // 4
+    work[:wide, wide:] = jnp.zeros((wide, wide), jnp.float32)
+    fill_lower(full, 0, work)
+
+    @pl.loop(0, 4)
+    def _(k):
+        start = pl.multiple_of(k * size, size)
+        at = pl.ds(start, size)
+
+        def act(second):
+            for n in range(4):
+
+                @pl.when(k == n)
+                def _():
+                    for action in actions[2 * n + second]:
+                        action()
+
+        done = factor_block(work[at, at], functools.partial(act, 0))
+        act(1)
+        lower = halves(done)
+        rows = lax.broadcasted_iota(jnp.int32, (whole, size), 0)
+        cols = lax.broadcasted_iota(jnp.int32, (size, whole), 1)
+        below = rows >= start + size
+        own = work[:, at]
+        column = jnp.where(below, triple(halves(own), lower, TURNED), 0.0)
+        known = jnp.where(cols < start, work[at, :], 0.0)
+        lead[at, :] = triple(lower, halves(known), PLAIN)
+        lead[at, at] = done
+        work[:, at] = jnp.where(below, 0.0, own)
+        pieces = halves(column)
+        work[...] -= triple(pieces, halves(lead[at, :]), PLAIN) + triple(pieces, pieces, TURNED)
 
 
 def square_factor(work, inverse, size, actions=()):

time: 228 us -> 208 us (0.912); the launches traced: 225 us -> 207 us
  Pallas kernels: 223 us -> 205 us
    pallas_call x1, Pallas kernels: 191 us -> 173 us  [filtered_sums(): pl.pallas_call(kernel, out_shape=[jax.ShapeDtypeStruct((panels, near_rows...]
where the time goes in v2:
time: 208 us; the launch traced here: 207 us
  Pallas kernels  205 us (99%)
    pallas_call x1, Pallas kernels, filtered_sums(): pl.pallas_call(kernel, out_shape=[jax.ShapeDtypeStruct((panels, near_rows...  173 us
    pallas_call x1, Pallas kernels, finish(): pl.pallas_call(functools.partial(finish_kernel, size, total_rows), out_sh...  32.3 us

profile of v2, /device:TPU:3, one launch (start us, length us, event | category | flops | bytes accessed | tf_op | source)
XLA Modules:
  0.0 207.1 jit_solution(13709347402040852278)
XLA Ops:
  0.0 0.8 copy.5
  0.8 0.7 select_add_fusion.refs_0_
  1.5 173.2 %shard_map.37 = (f32[4,576,256]{2,1,0:T(8,128)}, bf16[4,32,128,256]{3,2,1,0:T(8,128)(2,1)}, f32[512,512]{1,0:T(8,128)}) custom-call(s32[32,5]{1,0:T(8,128)} %select_add_fusion.refs_0_, bf16[32,128,256]{2,1,0:T(8,128)(2,1)} %bitcast.3, bf16[32,5,128,128]{3,2,1,0:T(8,128)(2,1)} %refs_2_.1), custom_call_target="tpu_custom_call" | custom-call | tf_op jit(solution)/shard_map/pallas_call | solution.py:648
  174.7 32.3 %shard_map.38 = f32[4096,256]{1,0:T(8,128)} custom-call(f32[4,576,256]{2,1,0:T(8,128)} %get-tuple-element.8.sums_ref, f32[512,512]{1,0:T(8,128)} %get-tuple-element.9.lead_ref, bf16[4,4096,256]{2,1,0:T(8,128)(2,1)} %bitcast.2), custom_call_target="tpu_custom_call" | custom-call | tf_op jit(solution)/shard_map/pallas_call | solution.py:883
  (3 shorter events, 0.0 us)
